TPU v7x, 768 devices: a whole 4x8x12 slice. The times are simulated.
768 devices in a mesh: ctx: 48 (over y, z_lo, core), dp: 16 (over x, z_hi).
Axes of the slice: x: 4, y: 8, z: 12 (z_hi: 4, z_lo: 3; z = z_hi * 3 + z_lo), core: 2. Of those that a mesh axis runs over, the one named last changes fastest.
Arguments:
- q_proj: bfloat16 [16, 6144, 2048], P('dp', 'ctx'), may hold values from -6 to 6
- k_proj: bfloat16 [16, 6144, 2048], P('dp', 'ctx'), may hold values from -6 to 6
- v_proj: bfloat16 [16, 6144, 2048], P('dp', 'ctx'), may hold values from -6 to 6
- out_grad: bfloat16 [16, 6144, 2048], P('dp', 'ctx'), may hold values from -6 to 6
- contig_starts: int32 [16, 6144], P('dp', 'ctx'), may hold values 0 or 1
- filters: bfloat16 [128, 128], replicated, may hold values from -0.5 to 0.5
Outputs:
- mixed_out: bfloat16 [16, 6144, 2048], P('dp', 'ctx')
- grad_q: bfloat16 [16, 6144, 2048], P('dp', 'ctx')
- grad_k: bfloat16 [16, 6144, 2048], P('dp', 'ctx')
- grad_v: bfloat16 [16, 6144, 2048], P('dp', 'ctx')
- filter_grad: float32 [128, 128], replicated
Inputs may be any that keep to these rules, and one draw needn't show every extreme that they name: `contig_starts`: a contig runs from a 1 to the token before the next 1 or to the end of its pack.
All inputs are finite; a program needn't handle non-finite values. No bound on the sum of `contig_starts` on one device may be relied on, other than what follows from the above.
Results may differ from a plain program's by a relative error of at most 0.0053.
Values may be sent and summed in bfloat16 or wider, within the bound.
A program may use at most 32 MiB of HBM per device.

v0:
```python
import math

import jax
import jax.numpy as jnp
from jax import lax
from jax.sharding import PartitionSpec as P

FILT = 128
GSIZE = 16


def passed_along(block, axis, distance):
    devices = range(lax.axis_size(axis))
    route = [(i - distance, i) for i in devices if i - distance in devices]
    return lax.ppermute(block, axis, route)


def skew_rows(row_table):
    count = row_table.shape[0]
    tiled = jnp.tile(row_table, (1, FILT))[:, : FILT * (2 * FILT - 1)]
    return tiled.reshape(count, FILT, 2 * FILT - 1)


def diagonal_sums(products):
    lead = products.shape[:-2]
    flat = products.reshape(lead + (FILT * (2 * FILT - 1),))
    flat = jnp.concatenate([flat, jnp.zeros(lead + (FILT,), flat.dtype)], axis=-1)
    return jnp.sum(flat.reshape(lead + (FILT, 2 * FILT))[..., :FILT], axis=-2)


def windows(extended):
    nblocks = extended.shape[0] // FILT - 1
    blocks = extended.reshape((nblocks + 1, FILT) + extended.shape[1:])
    return jnp.concatenate([blocks[:-1], blocks[1:, : FILT - 1]], axis=1)


def per_device(q_proj, k_proj, v_proj, out_grad, contig_starts, filters):
    queries = q_proj[0]
    keys_in = k_proj[0]
    values_in = v_proj[0]
    upstream = out_grad[0]
    rows = queries.shape[0]
    width = queries.shape[1]
    groups = filters.shape[0]
    nblocks = rows // FILT
    span = 2 * FILT - 1
    tail = FILT - 1
    per_step = math.gcd(groups, 8)
    chans = per_step * GSIZE
    segment_ids = jnp.cumsum(contig_starts[0])
    last_id = segment_ids[rows - 1]
    prod_kv = (keys_in.astype(jnp.float32) * values_in.astype(jnp.float32)).astype(jnp.bfloat16)
    cotangent = (upstream.astype(jnp.float32) * queries.astype(jnp.float32)).astype(jnp.bfloat16)
    tail_keep = segment_ids[rows - tail :] == last_id
    outgoing = prod_kv[rows - tail :] * tail_keep[:, None].astype(jnp.bfloat16)
    incoming = passed_along(outgoing, "ctx", 1)
    kv_ext = jnp.concatenate([incoming, prod_kv, jnp.zeros((1, width), jnp.bfloat16)], 0)
    seg_ext = jnp.concatenate(
        [jnp.zeros((tail,), jnp.int32), segment_ids, jnp.full((1,), -1, jnp.int32)], 0
    )
    kv_win = windows(kv_ext)
    seg_win = windows(seg_ext)
    seg_own = segment_ids.reshape(nblocks, FILT)
    fwd_mask = (seg_win[:, None, :] == seg_own[:, :, None]).astype(jnp.bfloat16)
    head_keep = segment_ids[:tail] == 0
    head = passed_along(cotangent[:tail] * head_keep[:, None].astype(jnp.bfloat16), "ctx", -1)
    cot_ext = jnp.concatenate([cotangent, head, jnp.zeros((1, width), jnp.bfloat16)], 0)
    segc_ext = jnp.concatenate(
        [segment_ids, jnp.zeros((tail,), jnp.int32) + last_id, jnp.full((1,), -1, jnp.int32)], 0
    )
    cot_win = windows(cot_ext)
    back_mask = (windows(segc_ext)[:, None, :] == seg_own[:, :, None]).astype(jnp.bfloat16)

    def group_block(index, carry):
        mixed, grad_q, grad_kv, partial_sum, filter_local = carry
        start = index * chans
        taps = lax.dynamic_slice_in_dim(filters, index * per_step, per_step, 0)
        fwd_table = skew_rows(jnp.concatenate([taps[:, ::-1], jnp.zeros_like(taps)], axis=1))
        fwd_masked = fwd_table[None] * fwd_mask[:, None]
        kv_block = lax.dynamic_slice_in_dim(kv_win, start, chans, 2).reshape(
            nblocks, span, per_step, GSIZE
        )
        conv = jnp.einsum(
            "bgts,bsgc->btgc", fwd_masked, kv_block, preferred_element_type=jnp.float32
        ).reshape(rows, chans)
        q_block = lax.dynamic_slice_in_dim(queries, start, chans, 1)
        up_block = lax.dynamic_slice_in_dim(upstream, start, chans, 1)
        cot_block = lax.dynamic_slice_in_dim(cotangent, start, chans, 1).reshape(
            nblocks, FILT, per_step, GSIZE
        )
        mixed = lax.dynamic_update_slice_in_dim(
            mixed, (q_block.astype(jnp.float32) * conv).astype(jnp.bfloat16), start, 1
        )
        grad_q = lax.dynamic_update_slice_in_dim(
            grad_q, (up_block.astype(jnp.float32) * conv).astype(jnp.bfloat16), start, 1
        )
        products = jnp.einsum(
            "btgc,bsgc->bgts", cot_block, kv_block, preferred_element_type=jnp.float32
        )
        products = products * fwd_mask[:, None].astype(jnp.float32)
        diag = jnp.sum(diagonal_sums(products), axis=0)[:, ::-1]
        filter_local = lax.dynamic_update_slice_in_dim(filter_local, diag, index * per_step, 0)
        back_table = skew_rows(jnp.concatenate([taps, jnp.zeros_like(taps)], axis=1))
        back_masked = back_table[None] * back_mask[:, None]
        cw_block = lax.dynamic_slice_in_dim(cot_win, start, chans, 2).reshape(
            nblocks, span, per_step, GSIZE
        )
        local = jnp.einsum(
            "bgsw,bwgc->bsgc", back_masked, cw_block, preferred_element_type=jnp.float32
        )
        grad_kv = lax.dynamic_update_slice_in_dim(grad_kv, local.reshape(rows, chans), start, 1)
        return (mixed, grad_q, grad_kv, partial_sum, filter_local)

    initial = (
        jnp.zeros((rows, width), jnp.bfloat16),
        jnp.zeros((rows, width), jnp.bfloat16),
        jnp.zeros((rows, width), jnp.float32),
        jnp.zeros((tail, width), jnp.float32),
        jnp.zeros((groups, FILT), jnp.float32),
    )
    mixed, grad_q, grad_kv, partial_sum, filter_local = lax.fori_loop(
        0, groups // per_step, group_block, initial
    )
    grad_k = (grad_kv * values_in.astype(jnp.float32)).astype(jnp.bfloat16)
    grad_v = (grad_kv * keys_in.astype(jnp.float32)).astype(jnp.bfloat16)
    filter_sum = lax.psum(filter_local, ("ctx", "dp"))
    scale = 1.0 / math.sqrt(rows * lax.axis_size("ctx") * lax.axis_size("dp") * GSIZE)
    filter_grad = filter_sum * scale
    return (mixed[None], grad_q[None], grad_k[None], grad_v[None], filter_grad)


def solution(mesh):
    placed = (
        P("dp", "ctx", None),
        P("dp", "ctx", None),
        P("dp", "ctx", None),
        P("dp", "ctx", None),
        P("dp", "ctx"),
        P(),
    )
    return jax.shard_map(
        per_device,
        mesh=mesh,
        in_specs=placed,
        out_specs=(
            P("dp", "ctx", None),
            P("dp", "ctx", None),
            P("dp", "ctx", None),
            P("dp", "ctx", None),
            P(),
        ),
        check_vma=False,
    )
```

profile of v0, /device:TPU:1, one launch (start us, length us, event | category | flops | bytes accessed | tf_op | source)
XLA Modules:
  0.0 657.3 jit_solution(3033199212600479855)
XLA Ops:
  11.4 12.4 %collective-permute-start.1 = (bf16[127,2048]{0,1:T(8,128)(2,1)}, bf16[127,2048]{0,1:T(8,128)(2,1)}, u32[]{:S(2)}, u32[]{:S(2)}) collective-permute-start(bf16[127,2048]{0,1:T(8,128)(2,1)} %slice_multiply_fusion), channel_id=1, source_target_pairs={{16,0},{32,16},{48,32},{64,48},{80,64},{96,80},{112,96},{128,112},... | collective-permute-start | bytes 1560584 | tf_op jit(solution)/shard_map/ppermute | solution.py:15
  25.0 1.9 collective-permute-start
  28.9 2.2 maximum_maximum_fusion.1
  31.1 2.2 reshape.302
  33.3 2.2 slice.103
  42.1 145.8 %while.21 = (s32[]{:T(128)}, bf16[128,2048]{1,0:T(8,128)(2,1)}, bf16[128,2048]{1,0:T(8,128)(2,1)}, f32[128,2048]{1,0:T(8,128)}, f32[128,128]{1,0:T(8,128)S(1)}, ...) while((s32[]{:T(128)}, bf16[128,2048]{1,0:T(8,128)(2,1)}, ...), condition=%wide.region_3.4_spmd.clone.clone, body=%wide.region_1.3_spmd.clone.clone.sunk | while | flops 26242440 | bytes 18328176 | solution.py:121
  44.0 1.4 reshape.335
  48.9 1.4 reshape.336
  53.1 1.4 reshape.335
  62.2 1.4 reshape.335
  67.1 1.4 reshape.336
  71.3 1.4 reshape.335
  76.2 1.4 reshape.336
  80.4 1.4 reshape.335
  85.3 1.4 reshape.336
  89.5 1.4 reshape.335
  94.4 1.4 reshape.336
  103.5 1.4 reshape.336
  107.8 1.4 reshape.335
  112.6 1.4 reshape.336
  116.9 1.4 reshape.335
  188.6 2.8 fusion.18
  191.3 457.7 %all-reduce.6.cloned.1.call-done = f32[128,128]{1,0:T(8,128)} async-done(((f32[128,128]{1,0:T(8,128)}), f32[128,128]{1,0:T(8,128)}) %all-reduce.6.cloned.1.call-update) | async-done | bytes 65552 | tf_op jit(solution)/shard_map/psum | solution.py:126
  649.0 1.5 broadcast_multiply_fusion
  (560 shorter events, 137.9 us)
Async XLA Ops:
  7.2 641.8 %all-reduce.6.cloned.1.call-start = ((), (), s32[]{:S(2)}) async-start(), calls=%async_computation | async-start | bytes 131072 | tf_op jit(solution)/shard_map/psum | solution.py:126
  10.4 13.4 %copy-start.2 = (bf16[1,128,2048]{2,1,0:T(8,128)(2,1)S(1)}, bf16[1,128,2048]{2,1,0:T(8,128)(2,1)}, u32[]{:S(2)}) copy-start(bf16[1,128,2048]{2,1,0:T(8,128)(2,1)} %param.9) | copy-start | bytes 1572868
  10.5 13.4 %copy-start.3 = (bf16[1,128,2048]{2,1,0:T(8,128)(2,1)S(1)}, bf16[1,128,2048]{2,1,0:T(8,128)(2,1)}, u32[]{:S(2)}) copy-start(bf16[1,128,2048]{2,1,0:T(8,128)(2,1)} %param.10) | copy-start | bytes 1572868
  11.4 17.4 %collective-permute-start.1 = (bf16[127,2048]{0,1:T(8,128)(2,1)}, bf16[127,2048]{0,1:T(8,128)(2,1)}, u32[]{:S(2)}, u32[]{:S(2)}) collective-permute-start(bf16[127,2048]{0,1:T(8,128)(2,1)} %slice_multiply_fusion), channel_id=1, source_target_pairs={{16,0},{32,16},{48,32},{64,48},{80,64},{96,80},{112,96},{128,112},... | collective-permute-start | bytes 1560584 | tf_op jit(solution)/shard_map/ppermute | solution.py:15
  25.0 10.6 %collective-permute-start = (bf16[127,2048]{1,0:T(8,128)(2,1)}, bf16[127,2048]{1,0:T(8,128)(2,1)S(1)}, u32[]{:S(2)}, u32[]{:S(2)}) collective-permute-start(bf16[127,2048]{1,0:T(8,128)(2,1)} %slice_multiply_fusion.1), channel_id=1, source_target_pairs={{0,16},{16,32},{32,48},{48,64},{64,80},{80,96},{96,112},{112,128},... | collective-permute-start | bytes 1560584 | tf_op jit(solution)/shard_map/ppermute | solution.py:15
  42.1 4.6 copy-start
  51.3 4.5 copy-start
  60.4 4.5 copy-start
  69.5 4.5 copy-start
  78.5 4.5 copy-start
  87.7 4.5 copy-start
  94.4 2.4 copy-start.1
  96.8 4.5 copy-start
  105.9 4.5 copy-start
  112.6 2.4 copy-start.1
  115.0 4.5 copy-start
  124.2 4.5 copy-start
  133.3 4.5 copy-start
  142.4 4.5 copy-start
  149.1 2.4 copy-start.1
  151.5 4.5 copy-start
  160.6 4.5 copy-start
  169.7 4.5 copy-start
  178.8 4.5 copy-start
  (17 other events, 35.9 us)
Sparse Core Ops, SparseCore 0:
  188.7 460.2 all-reduce.5
where the time goes:
time: 661 us; the launch traced here: 657 us
  waiting for transfers between devices  458 us (69%)
  local copies, waits for them, and re-layouts  138 us (21%)
  other arithmetic  17.4 us (3%)
  starting transfers between devices  14.3 us (2%)
  between operations  14.2 us (2%)
  matrix products  13.3 us (2%)
    psum x1, waiting for transfers between devices, per_device(): filter_sum = lax.psum(filter_local, ('ctx', 'dp'))  458 us
    reshape x16, local copies, waits for them, and re-layouts, group_block(): fwd_masked = fwd_table[None] * fwd_mask[:, None]  21.8 us
    reshape x16, local copies, waits for them, and re-layouts, group_block(): back_masked = back_table[None] * back_mask[:, None]  21.8 us
    dynamic_slice x32, local copies, waits for them, and re-layouts, group_block(): lax.dynamic_slice_in_dim(kv_win, start, chans, 2)  16 us
    ppermute x2, starting transfers between devices, passed_along(): return lax.ppermute(block, axis, route)  14.3 us
    dynamic_slice x16, local copies, waits for them, and re-layouts, group_block(): lax.dynamic_slice_in_dim(cot_win, start, chans, 2)  13.5 us
  transfers between devices with their start and end apart: 3, of which 1 were waited for; matrix products, arithmetic and copies ran while one was open for 2% of the time, Pallas kernels for 0%

commit v1 on v0

v1 whole, which is shorter than its diff:
```python
import functools
import math

import jax
import jax.numpy as jnp
from jax import lax
from jax.experimental import pallas as pl
from jax.experimental.pallas import tpu as pltpu
from jax.sharding import PartitionSpec as P

FILT = 128
GSIZE = 16
LANES = 128
PER_TILE = LANES // GSIZE
SUB = 8
CORES = 2
Z_LO = 3
Z_HI = 4
CHUNK = 4
MESH = pl.DeviceIdType.MESH
F32 = jnp.float32
BF16 = jnp.bfloat16


def ring_kernel(
    n_ctx,
    n_dp,
    scale,
    q_hbm,
    k_hbm,
    v_hbm,
    dy_hbm,
    starts_ref,
    filt_ref,
    mixed_hbm,
    gq_hbm,
    gk_hbm,
    gv_hbm,
    fg_ref,
    q,
    k,
    v,
    dy,
    kvx,
    cotx,
    kvs,
    cots,
    lhs,
    lane_mask,
    masks,
    pair_mask,
    fil,
    rfil,
    fold,
    filt_rev,
    filt_local,
    slots1,
    slots2,
    slots3,
    acc1,
    acc2,
    acc3,
    gathered,
    mixed,
    gq,
    gk,
    gv,
    in_sem,
    out_sem,
    kv_send,
    kv_recv,
    cot_send,
    cot_recv,
    s1_send,
    s1_recv,
    s2_send,
    s2_recv,
    s3_send,
    s3_recv,
    s4_send,
    s4_recv,
):
    ctx = lax.axis_index("ctx")
    dp = lax.axis_index("dp")
    core = lax.rem(ctx, CORES)
    z_lo = lax.rem(ctx // CORES, Z_LO)
    y = ctx // (CORES * Z_LO)
    z_hi = lax.rem(dp, Z_HI)
    x = dp // Z_HI
    n_y = n_ctx // (CORES * Z_LO)
    n_x = n_dp // Z_HI
    n_plane = n_x * CORES
    n_z = Z_LO * Z_HI
    me1 = x * CORES + core
    me3 = z_hi * Z_LO + z_lo
    tiles = kvx.shape[0]
    n_chunks = tiles // CHUNK
    share = filt_local.shape[0] // n_plane

    def plane_peer(p):
        return {"ctx": ctx - core + lax.rem(p, CORES), "dp": (p // CORES) * Z_HI + z_hi}

    def y_peer(p):
        return {"ctx": p * (CORES * Z_LO) + z_lo * CORES + core, "dp": dp}

    def z_peer(p):
        return {
            "ctx": y * (CORES * Z_LO) + lax.rem(p, Z_LO) * CORES + core,
            "dp": x * Z_HI + p // Z_LO,
        }

    nxt = {"ctx": lax.rem(ctx + 1, n_ctx), "dp": dp}
    prv = {"ctx": lax.rem(ctx + n_ctx - 1, n_ctx), "dp": dp}

    loads = [
        pltpu.make_async_copy(src, dst, in_sem.at[i])
        for i, (src, dst) in enumerate(((k_hbm, k), (v_hbm, v), (q_hbm, q), (dy_hbm, dy)))
    ]
    for copy in loads:
        copy.start()

    barrier = pltpu.get_barrier_semaphore()

    def greet(device):
        pl.semaphore_signal(barrier, inc=1, device_id=device, device_id_type=MESH)

    def greet_all(n, me, peer):
        def one(d, carry):
            greet(peer(lax.rem(me + d, n)))
            return carry

        lax.fori_loop(1, n, one, 0)

    greet(nxt)
    greet(prv)
    greet_all(n_z, me3, z_peer)
    greet_all(n_y, y, y_peer)
    greet_all(n_plane, me1, plane_peer)

    row = lax.broadcasted_iota(jnp.int32, (FILT, FILT), 0)
    col = lax.broadcasted_iota(jnp.int32, (FILT, FILT), 1)
    starts = starts_ref[...].astype(F32)
    seg_row = jnp.broadcast_to(
        jnp.sum(jnp.where(col <= row, starts, 0.0), axis=1, keepdims=True), (FILT, FILT)
    )
    seg_col = seg_row.T
    last = jnp.sum(starts)
    same = seg_row == seg_col
    fresh = seg_row == 0.0
    final = seg_row == last

    def held(cond):
        return jnp.where(cond, 1.0, 0.0)

    low = held(same & (col <= row))
    high = held(fresh & (col > row))
    pair_mask[...] = low + high
    masks[0] = high.astype(BF16)
    masks[1] = low.astype(BF16)
    masks[2] = held(same & (row <= col)).astype(BF16)
    masks[3] = held(final & (col < row)).astype(BF16)
    masks[4] = (held(final) * jnp.where(ctx == n_ctx - 1, 0.0, 1.0)).astype(BF16)
    masks[5] = (held(fresh) * jnp.where(ctx == 0, 0.0, 1.0)).astype(BF16)
    lane_group = col // GSIZE
    for g in range(PER_TILE):
        lane_mask[g] = held(lane_group == g).astype(BF16)
    mirror = held(row == lax.rem(FILT - col, FILT))
    taps = filt_ref[...]
    fil[...] = taps.astype(F32)
    rfil[...] = jnp.dot(taps, mirror.astype(BF16), preferred_element_type=F32)

    def lanes_of(j):
        return pl.ds(pl.multiple_of(j * LANES, LANES), LANES)

    loads[0].wait()
    loads[1].wait()

    def make_kv(j, carry):
        lanes = lanes_of(j)
        prod = (k[:, lanes].astype(F32) * v[:, lanes].astype(F32)).astype(BF16)
        kvx[j, FILT:, :] = prod
        kvs[j] = prod * masks[4]
        return carry

    lax.fori_loop(0, tiles, make_kv, 0)

    pl.semaphore_wait(barrier, 2 + (n_z - 1) + (n_y - 1) + (n_plane - 1))

    def kv_copy(i):
        part = pl.ds(i * CHUNK, CHUNK)
        return pltpu.make_async_remote_copy(
            src_ref=kvs.at[part],
            dst_ref=kvx.at[part, 0:FILT, :],
            send_sem=kv_send.at[i],
            recv_sem=kv_recv.at[i],
            device_id=nxt,
            device_id_type=MESH,
        )

    def cot_copy(i):
        part = pl.ds(i * CHUNK, CHUNK)
        return pltpu.make_async_remote_copy(
            src_ref=cots.at[part],
            dst_ref=cotx.at[part, FILT:, :],
            send_sem=cot_send.at[i],
            recv_sem=cot_recv.at[i],
            device_id=prv,
            device_id_type=MESH,
        )

    for i in range(n_chunks):
        kv_copy(i).start()

    loads[2].wait()
    loads[3].wait()

    def make_cot(j, carry):
        lanes = lanes_of(j)
        prod = (dy[:, lanes].astype(F32) * q[:, lanes].astype(F32)).astype(BF16)
        cotx[j, 0:FILT, :] = prod
        cots[j] = prod * masks[5]
        return carry

    lax.fori_loop(0, tiles, make_cot, 0)

    def products(j, carry):
        cot = cotx[j, 0:FILT, :]
        for g in range(PER_TILE):
            lhs[g * FILT : (g + 1) * FILT, 0:LANES] = cot * lane_mask[g]
        pairs = lax.dot_general(
            lhs[:, 0:LANES], kvx[j], (((1,), (1,)), ((), ())), preferred_element_type=F32
        )
        for g in range(PER_TILE):
            block = pairs[g * FILT : (g + 1) * FILT]
            square = jnp.where(col <= row, block[:, FILT:], block[:, :FILT]) * pair_mask[...]
            folded = square[0:SUB]
            for a in range(1, FILT // SUB):
                folded = folded + pltpu.roll(square[a * SUB : (a + 1) * SUB], FILT - a * SUB, 1)
            fold[g] = folded
        taps8 = fold[:, 0, :]
        for b in range(1, SUB):
            taps8 = taps8 + pltpu.roll(fold[:, b, :], FILT - b, 1)
        filt_rev[pl.ds(pl.multiple_of(j * PER_TILE, PER_TILE), PER_TILE), :] = taps8
        return carry

    for i in range(n_chunks):
        kv_copy(i).wait_recv()
        if i == n_chunks - 1:
            for c in range(n_chunks):
                cot_copy(c).start()
        lax.fori_loop(i * CHUNK, (i + 1) * CHUNK, products, 0)

    filt_local[...] = lax.dot_general(
        filt_rev[...],
        mirror,
        (((1,), (0,)), ((), ())),
        precision=lax.Precision.HIGHEST,
        preferred_element_type=F32,
    )

    def send_all(n, me, peer, src_of, dst, send, recv):
        def one(d, carry):
            p = lax.rem(me + d, n)
            pltpu.make_async_remote_copy(
                src_ref=src_of(p),
                dst_ref=dst(me),
                send_sem=send.at[p],
                recv_sem=recv.at[me],
                device_id=peer(p),
                device_id_type=MESH,
            ).start()
            return carry

        lax.fori_loop(1, n, one, 0)

    def await_all(n, me, peer, src_of, dst, send, recv, sent):
        def one(d, carry):
            p = lax.rem(me + d, n)
            copy = pltpu.make_async_remote_copy(
                src_ref=src_of(p),
                dst_ref=dst(p),
                send_sem=send.at[p],
                recv_sem=recv.at[p],
                device_id=peer(p),
                device_id_type=MESH,
            )
            if sent:
                copy.wait_send()
            else:
                copy.wait_recv()
            return carry

        lax.fori_loop(1, n, one, 0)

    def share_of(ref, p):
        return ref.at[pl.ds(pl.multiple_of(p * share, share), share)]

    stage1 = (n_plane, me1, plane_peer, lambda p: share_of(filt_local, p), lambda p: slots1.at[p], s1_send, s1_recv)
    stage2 = (n_y, y, y_peer, lambda p: acc1, lambda p: slots2.at[p], s2_send, s2_recv)
    stage3 = (n_z, me3, z_peer, lambda p: acc2, lambda p: slots3.at[p], s3_send, s3_recv)
    stage4 = (n_plane, me1, plane_peer, lambda p: acc3, lambda p: share_of(gathered, p), s4_send, s4_recv)

    def total(slots, n):
        result = slots[0]
        for i in range(1, n):
            result = result + slots[i]
        return result

    lane_of = lax.broadcasted_iota(jnp.int32, (FILT, LANES), 1) // GSIZE

    def table(rows8, first, second):
        for g in range(PER_TILE):
            base = jnp.broadcast_to(rows8[g : g + 1, :], (FILT, FILT))
            circ = pltpu.roll(base, 0, 1, stride=1, stride_axis=0).astype(BF16)
            lhs[g * FILT : (g + 1) * FILT, 0:FILT] = circ * masks[first]
            lhs[g * FILT : (g + 1) * FILT, FILT:] = circ * masks[second]

    def apply_table(operand):
        result = jnp.dot(lhs[...], operand, preferred_element_type=F32)
        out = result[0:FILT]
        for g in range(1, PER_TILE):
            out = jnp.where(lane_of == g, result[g * FILT : (g + 1) * FILT], out)
        return out

    def forward(j, carry):
        lanes = lanes_of(j)
        rows8 = rfil[pl.ds(pl.multiple_of(j * PER_TILE, PER_TILE), PER_TILE), :]
        table(rows8, 0, 1)
        conv = apply_table(kvx[j])
        mixed[:, lanes] = (q[:, lanes].astype(F32) * conv).astype(BF16)
        gq[:, lanes] = (dy[:, lanes].astype(F32) * conv).astype(BF16)
        return carry

    def backward(j, carry):
        lanes = lanes_of(j)
        rows8 = fil[pl.ds(pl.multiple_of(j * PER_TILE, PER_TILE), PER_TILE), :]
        table(rows8, 2, 3)
        grad = apply_table(cotx[j])
        gk[:, lanes] = (v[:, lanes].astype(F32) * grad).astype(BF16)
        gv[:, lanes] = (k[:, lanes].astype(F32) * grad).astype(BF16)
        return carry

    send_all(*stage1)
    slots1[me1] = filt_local[pl.ds(pl.multiple_of(me1 * share, share), share), :]
    lax.fori_loop(0, tiles // 2, forward, 0)
    await_all(*stage1, False)
    acc1[...] = total(slots1, n_plane)
    send_all(*stage2)
    slots2[y] = acc1[...]
    lax.fori_loop(tiles // 2, tiles, forward, 0)
    stores = [
        pltpu.make_async_copy(src, dst, out_sem.at[i])
        for i, (src, dst) in enumerate(((mixed, mixed_hbm), (gq, gq_hbm), (gk, gk_hbm), (gv, gv_hbm)))
    ]
    stores[0].start()
    stores[1].start()
    await_all(*stage2, False)
    acc2[...] = total(slots2, n_y)
    send_all(*stage3)
    slots3[me3] = acc2[...]
    for i in range(n_chunks):
        cot_copy(i).wait_recv()
        lax.fori_loop(i * CHUNK, (i + 1) * CHUNK, backward, 0)
    stores[2].start()
    stores[3].start()
    await_all(*stage3, False)
    acc3[...] = total(slots3, n_z)
    send_all(*stage4)
    gathered[pl.ds(pl.multiple_of(me1 * share, share), share), :] = acc3[...]
    for i in range(n_chunks):
        kv_copy(i).wait_send()
        cot_copy(i).wait_send()
    await_all(*stage1, True)
    await_all(*stage2, True)
    await_all(*stage3, True)
    for copy in stores:
        copy.wait()
    await_all(*stage4, False)
    fg_ref[...] = gathered[...] * scale
    await_all(*stage4, True)


def per_device(n_ctx, n_dp, q_proj, k_proj, v_proj, out_grad, contig_starts, filters):
    rows, width = q_proj.shape[1:]
    groups = filters.shape[0]
    tiles = width // LANES
    n_y = n_ctx // (CORES * Z_LO)
    n_plane = (n_dp // Z_HI) * CORES
    n_z = Z_LO * Z_HI
    share = groups // n_plane
    n_chunks = tiles // CHUNK
    scale = 1.0 / math.sqrt(rows * n_ctx * n_dp * GSIZE)
    any_spec = pl.BlockSpec(memory_space=pl.ANY)
    vmem_spec = pl.BlockSpec(memory_space=pltpu.VMEM)
    big = jax.ShapeDtypeStruct((rows, width), BF16)
    dma = pltpu.SemaphoreType.DMA
    wide = pltpu.VMEM((rows, width), BF16)
    mixed, grad_q, grad_k, grad_v, filter_grad = pl.pallas_call(
        functools.partial(ring_kernel, n_ctx, n_dp, scale),
        out_shape=(big, big, big, big, jax.ShapeDtypeStruct((groups, FILT), F32)),
        in_specs=[any_spec] * 4 + [vmem_spec] * 2,
        out_specs=(any_spec, any_spec, any_spec, any_spec, vmem_spec),
        scratch_shapes=[
            wide,
            wide,
            wide,
            wide,
            pltpu.VMEM((tiles, 2 * FILT, LANES), BF16),
            pltpu.VMEM((tiles, 2 * FILT, LANES), BF16),
            pltpu.VMEM((tiles, FILT, LANES), BF16),
            pltpu.VMEM((tiles, FILT, LANES), BF16),
            pltpu.VMEM((PER_TILE * FILT, 2 * FILT), BF16),
            pltpu.VMEM((PER_TILE, FILT, LANES), BF16),
            pltpu.VMEM((6, FILT, FILT), BF16),
            pltpu.VMEM((FILT, FILT), F32),
            pltpu.VMEM((groups, FILT), F32),
            pltpu.VMEM((groups, FILT), F32),
            pltpu.VMEM((PER_TILE, SUB, FILT), F32),
            pltpu.VMEM((groups, FILT), F32),
            pltpu.VMEM((groups, FILT), F32),
            pltpu.VMEM((n_plane, share, FILT), F32),
            pltpu.VMEM((n_y, share, FILT), F32),
            pltpu.VMEM((n_z, share, FILT), F32),
            pltpu.VMEM((share, FILT), F32),
            pltpu.VMEM((share, FILT), F32),
            pltpu.VMEM((share, FILT), F32),
            pltpu.VMEM((groups, FILT), F32),
            wide,
            wide,
            wide,
            wide,
            dma((4,)),
            dma((4,)),
            dma((n_chunks,)),
            dma((n_chunks,)),
            dma((n_chunks,)),
            dma((n_chunks,)),
            dma((n_plane,)),
            dma((n_plane,)),
            dma((n_y,)),
            dma((n_y,)),
            dma((n_z,)),
            dma((n_z,)),
            dma((n_plane,)),
            dma((n_plane,)),
        ],
        compiler_params=pltpu.CompilerParams(collective_id=0, has_side_effects=True),
    )(q_proj[0], k_proj[0], v_proj[0], out_grad[0], contig_starts, filters)
    return (mixed[None], grad_q[None], grad_k[None], grad_v[None], filter_grad)


def solution(mesh):
    split = P("dp", "ctx", None)
    return jax.shard_map(
        functools.partial(per_device, mesh.shape["ctx"], mesh.shape["dp"]),
        mesh=mesh,
        in_specs=(split, split, split, split, P("dp", "ctx"), P()),
        out_specs=(split, split, split, split, P()),
        check_vma=False,
    )
```

time: 661 us -> 60.7 us (0.09)
  waiting for transfers between devices: 458 us -> 0 us
  local copies, waits for them, and re-layouts: 138 us -> 5.89 us
  Pallas kernels: 0 us -> 53.7 us
  other arithmetic: 17.4 us -> 0 us
  starting transfers between devices: 14.3 us -> 0 us
  between operations: 14.2 us -> 0.65 us
  matrix products: 13.3 us -> 0 us
    psum x1 -> x0, waiting for transfers between devices: 458 us -> none  [per_device(): filter_sum = lax.psum(filter_local, ('ctx', 'dp'))]
    reshape x49 -> x0, local copies, waits for them, and re-layouts: 55.6 us -> none  [the longest x16 21.8 us: group_block(): fwd_masked = fwd_table[None] * fwd_mask[:, None]]
    pallas_call x0 -> x1, Pallas kernels: none -> 53.7 us  [per_device(): pl.pallas_call(functools.partial(ring_kernel, n_ctx, n_dp, scale), out_sh...]
    dynamic_slice x80 -> x0, local copies, waits for them, and re-layouts: 40.6 us -> none  [the longest x32 16 us: group_block(): lax.dynamic_slice_in_dim(kv_win, start, chans, 2)]
    dynamic_update_slice x96 -> x0, local copies, waits for them, and re-layouts: 26.1 us -> none  [the longest x32 12.1 us: group_block(): lax.dynamic_update_slice_in_dim(grad_kv, local.reshape(rows, chans), star...]
    ppermute x2 -> x0, starting transfers between devices: 14.3 us -> none  [passed_along(): return lax.ppermute(block, axis, route)]
    dot_general x48 -> x0, matrix products: 13.3 us -> none  [the longest x16 5.52 us: group_block(): jnp.einsum('btgc,bsgc->bgts', cot_block, kv_block, preferred_element_type...]
  transfers between devices with their start and end apart: 3 -> 0, of which waited for: 1 -> 0; matrix products, arithmetic and copies ran while one was open for 2% -> 0% of each run, Pallas kernels for 0% -> 0%
where the time goes in v1:
time: 60.7 us; the launch traced here: 60.3 us
  Pallas kernels  53.7 us (88%)
  local copies, waits for them, and re-layouts  5.89 us (10%)
  between operations  0.65 us (1%)
    pallas_call x1, Pallas kernels, per_device(): pl.pallas_call(functools.partial(ring_kernel, n_ctx, n_dp, scale), out_sh...  53.7 us
    unnamed x13, local copies, waits for them, and re-layouts  5.89 us

profile of v1, /device:TPU:1, one launch (start us, length us, event | category | flops | bytes accessed | tf_op | source)
XLA Modules:
  0.0 60.3 jit_solution(8081287221442067032)
XLA Ops:
  0.6 53.7 %shard_map.101 = (bf16[128,2048]{1,0:T(8,128)(2,1)}, bf16[128,2048]{1,0:T(8,128)(2,1)}, bf16[128,2048]{1,0:T(8,128)(2,1)}, bf16[128,2048]{1,0:T(8,128)(2,1)}, f32[128,128]{1,0:T(8,128)}) custom-call(bf16[128,2048]{1,0:T(8,128)(2,1)} %bitcast.8, bf16[128,2048]{1,0:T(8,128)(2,1)} %bitcast.9, bf16[128,2048]{1,0:T(8,128)(2,1)} %bitcast.10, ...), custom_call_target="tpu_custom_call" | custom-call | tf_op jit(solution)/shard_map/pallas_call | solution.py:398
  54.4 0.0 copy-start.2
  54.4 1.9 %copy.16 = bf16[1,128,2048]{2,1,0:T(8,128)(2,1)} copy(bf16[1,128,2048]{2,1,0:T(8,128)(2,1)} %bitcast.15) | data formatting | bytes 1048576
  56.3 0.0 copy-done.2
  56.3 0.0 copy-start.1
  56.3 0.8 %copy.17 = bf16[1,128,2048]{2,1,0:T(8,128)(2,1)} copy(bf16[1,128,2048]{2,1,0:T(8,128)(2,1)S(1)} %bitcast.14) | data formatting | bytes 1048576
  57.1 0.4 copy-done.1
  57.5 0.0 copy-start
  57.5 0.8 %copy.18 = bf16[1,128,2048]{2,1,0:T(8,128)(2,1)} copy(bf16[1,128,2048]{2,1,0:T(8,128)(2,1)S(1)} %bitcast.13) | data formatting | bytes 1048576
  58.3 0.4 copy-done
  58.8 0.0 copy-start.3
  58.8 0.8 %copy.19 = bf16[1,128,2048]{2,1,0:T(8,128)(2,1)} copy(bf16[1,128,2048]{2,1,0:T(8,128)(2,1)S(1)} %bitcast.12) | data formatting | bytes 1048576
  59.6 0.1 copy-done.3
  59.6 0.6 %copy.20 = f32[128,128]{1,0:T(8,128)} copy(f32[128,128]{1,0:T(8,128)S(1)} %copy-done.3) | data formatting | bytes 131072
Async XLA Ops:
  54.4 2.0 %copy-start.2 = (bf16[128,2048]{1,0:T(8,128)(2,1)S(1)}, bf16[128,2048]{1,0:T(8,128)(2,1)}, u32[]{:S(2)}) copy-start(bf16[128,2048]{1,0:T(8,128)(2,1)} %get-tuple-element.11) | copy-start | bytes 1572868
  56.3 1.2 %copy-start.1 = (bf16[128,2048]{1,0:T(8,128)(2,1)S(1)}, bf16[128,2048]{1,0:T(8,128)(2,1)}, u32[]{:S(2)}) copy-start(bf16[128,2048]{1,0:T(8,128)(2,1)} %get-tuple-element.12) | copy-start | bytes 1572868
  57.5 1.2 %copy-start = (bf16[128,2048]{1,0:T(8,128)(2,1)S(1)}, bf16[128,2048]{1,0:T(8,128)(2,1)}, u32[]{:S(2)}) copy-start(bf16[128,2048]{1,0:T(8,128)(2,1)} %get-tuple-element.13) | copy-start | bytes 1572868
  58.8 0.9 %copy-start.3 = (f32[128,128]{1,0:T(8,128)S(1)}, f32[128,128]{1,0:T(8,128)}, u32[]{:S(2)}) copy-start(f32[128,128]{1,0:T(8,128)} %get-tuple-element.24) | copy-start | bytes 196612

commit v2 on v1

--- a/solution.py
+++ b/solution.py
@@ -16,7 +16,9 @@
 CORES = 2
 Z_LO = 3
 Z_HI = 4
-CHUNK = 4
+CHUNK = 2
+COT_CHUNK = 4
+PARTS = 2
 MESH = pl.DeviceIdType.MESH
 F32 = jnp.float32
 BF16 = jnp.bfloat16
@@ -32,10 +34,10 @@
     dy_hbm,
     starts_ref,
     filt_ref,
-    mixed_hbm,
-    gq_hbm,
-    gk_hbm,
-    gv_hbm,
+    mixed,
+    gq,
+    gk,
+    gv,
     fg_ref,
     q,
     k,
@@ -61,12 +63,7 @@
     acc2,
     acc3,
     gathered,
-    mixed,
-    gq,
-    gk,
-    gv,
     in_sem,
-    out_sem,
     kv_send,
     kv_recv,
     cot_send,
@@ -79,6 +76,7 @@
     s3_recv,
     s4_send,
     s4_recv,
+    heard,
 ):
     ctx = lax.axis_index("ctx")
     dp = lax.axis_index("dp")
@@ -95,7 +93,10 @@
     me3 = z_hi * Z_LO + z_lo
     tiles = kvx.shape[0]
     n_chunks = tiles // CHUNK
-    share = filt_local.shape[0] // n_plane
+    n_cot = tiles // COT_CHUNK
+    share = filt_local.shape[0] // (n_plane * PARTS)
+    part_groups = filt_local.shape[0] // PARTS
+    part_chunks = n_chunks // PARTS
 
     def plane_peer(p):
         return {"ctx": ctx - core + lax.rem(p, CORES), "dp": (p // CORES) * Z_HI + z_hi}
@@ -131,11 +132,27 @@
 
         lax.fori_loop(1, n, one, 0)
 
+    def z_step(d):
+        return z_peer(lax.rem(me3 + d + n_z, n_z))
+
+    z_near = [d for d in (1, -1) if n_z > 1]
+    z_far = [d for d in (2, -2) if n_z > 3]
+    greet_all(n_y, y, y_peer)
     greet(nxt)
     greet(prv)
-    greet_all(n_z, me3, z_peer)
-    greet_all(n_y, y, y_peer)
+    for d in z_near:
+        greet(z_step(d))
     greet_all(n_plane, me1, plane_peer)
+
+    def tell(stage, steps):
+        for d in steps:
+            pl.semaphore_signal(
+                heard.at[stage], inc=1, device_id=z_step(d), device_id_type=MESH
+            )
+
+    def hear(stage, steps):
+        if steps:
+            pl.semaphore_wait(heard.at[stage], len(steps))
 
     row = lax.broadcasted_iota(jnp.int32, (FILT, FILT), 0)
     col = lax.broadcasted_iota(jnp.int32, (FILT, FILT), 1)
@@ -184,25 +201,25 @@
 
     lax.fori_loop(0, tiles, make_kv, 0)
 
-    pl.semaphore_wait(barrier, 2 + (n_z - 1) + (n_y - 1) + (n_plane - 1))
+    pl.semaphore_wait(barrier, 2 + len(z_near) + (n_y - 1) + (n_plane - 1))
 
     def kv_copy(i):
         part = pl.ds(i * CHUNK, CHUNK)
         return pltpu.make_async_remote_copy(
             src_ref=kvs.at[part],
             dst_ref=kvx.at[part, 0:FILT, :],
-            send_sem=kv_send.at[i],
+            send_sem=kv_send,
             recv_sem=kv_recv.at[i],
             device_id=nxt,
             device_id_type=MESH,
         )
 
     def cot_copy(i):
-        part = pl.ds(i * CHUNK, CHUNK)
+        part = pl.ds(i * COT_CHUNK, COT_CHUNK)
         return pltpu.make_async_remote_copy(
             src_ref=cots.at[part],
             dst_ref=cotx.at[part, FILT:, :],
-            send_sem=cot_send.at[i],
+            send_sem=cot_send,
             recv_sem=cot_recv.at[i],
             device_id=prv,
             device_id_type=MESH,
@@ -210,6 +227,7 @@
 
     for i in range(n_chunks):
         kv_copy(i).start()
+    tell(0, z_near)
 
     loads[2].wait()
     loads[3].wait()
@@ -243,29 +261,14 @@
         filt_rev[pl.ds(pl.multiple_of(j * PER_TILE, PER_TILE), PER_TILE), :] = taps8
         return carry
 
-    for i in range(n_chunks):
-        kv_copy(i).wait_recv()
-        if i == n_chunks - 1:
-            for c in range(n_chunks):
-                cot_copy(c).start()
-        lax.fori_loop(i * CHUNK, (i + 1) * CHUNK, products, 0)
-
-    filt_local[...] = lax.dot_general(
-        filt_rev[...],
-        mirror,
-        (((1,), (0,)), ((), ())),
-        precision=lax.Precision.HIGHEST,
-        preferred_element_type=F32,
-    )
-
-    def send_all(n, me, peer, src_of, dst, send, recv):
+    def send_all(h, n, me, peer, src_of, dst, landed, send, recv):
         def one(d, carry):
             p = lax.rem(me + d, n)
             pltpu.make_async_remote_copy(
-                src_ref=src_of(p),
-                dst_ref=dst(me),
-                send_sem=send.at[p],
-                recv_sem=recv.at[me],
+                src_ref=src_of(h, p),
+                dst_ref=dst(h, me),
+                send_sem=send,
+                recv_sem=recv.at[h],
                 device_id=peer(p),
                 device_id_type=MESH,
             ).start()
@@ -273,38 +276,74 @@
 
         lax.fori_loop(1, n, one, 0)
 
-    def await_all(n, me, peer, src_of, dst, send, recv, sent):
-        def one(d, carry):
-            p = lax.rem(me + d, n)
-            copy = pltpu.make_async_remote_copy(
-                src_ref=src_of(p),
-                dst_ref=dst(p),
-                send_sem=send.at[p],
-                recv_sem=recv.at[p],
-                device_id=peer(p),
-                device_id_type=MESH,
-            )
-            if sent:
-                copy.wait_send()
-            else:
-                copy.wait_recv()
-            return carry
-
-        lax.fori_loop(1, n, one, 0)
-
-    def share_of(ref, p):
-        return ref.at[pl.ds(pl.multiple_of(p * share, share), share)]
-
-    stage1 = (n_plane, me1, plane_peer, lambda p: share_of(filt_local, p), lambda p: slots1.at[p], s1_send, s1_recv)
-    stage2 = (n_y, y, y_peer, lambda p: acc1, lambda p: slots2.at[p], s2_send, s2_recv)
-    stage3 = (n_z, me3, z_peer, lambda p: acc2, lambda p: slots3.at[p], s3_send, s3_recv)
-    stage4 = (n_plane, me1, plane_peer, lambda p: acc3, lambda p: share_of(gathered, p), s4_send, s4_recv)
-
-    def total(slots, n):
-        result = slots[0]
+    def everything(part, send, recv):
+        return pltpu.make_async_remote_copy(
+            src_ref=part,
+            dst_ref=part,
+            send_sem=send,
+            recv_sem=recv,
+            device_id=nxt,
+            device_id_type=MESH,
+        )
+
+    def await_part(h, n, me, peer, src_of, dst, landed, send, recv):
+        everything(landed.at[h, pl.ds(0, n - 1)], send, recv.at[h]).wait_recv()
+
+    def await_sent(n, me, peer, src_of, dst, landed, send, recv):
+        everything(landed.at[:, pl.ds(0, n - 1)], send, recv.at[0]).wait_send()
+
+    def rows_of(h, p):
+        return pl.ds(pl.multiple_of(h * part_groups + p * share, share), share)
+
+    def share_of(ref):
+        return lambda h, p: ref.at[rows_of(h, p)]
+
+    def slot_of(ref):
+        return lambda h, p: ref.at[h, p]
+
+    def whole(ref):
+        return lambda h, p: ref.at[h]
+
+    stage1 = (n_plane, me1, plane_peer, share_of(filt_local), slot_of(slots1), slots1, s1_send, s1_recv)
+    stage2 = (n_y, y, y_peer, whole(acc1), slot_of(slots2), slots2, s2_send, s2_recv)
+    stage3 = (n_z, me3, z_peer, whole(acc2), slot_of(slots3), slots3, s3_send, s3_recv)
+    stage4 = (n_plane, me1, plane_peer, whole(acc3), slot_of(gathered), gathered, s4_send, s4_recv)
+
+    def total(slots, h, n):
+        result = slots[h, 0]
         for i in range(1, n):
-            result = result + slots[i]
+            result = result + slots[h, i]
         return result
+
+    def begin(h):
+        span = slice(h * part_groups, (h + 1) * part_groups)
+        filt_local[span, :] = lax.dot_general(
+            filt_rev[span, :],
+            mirror,
+            (((1,), (0,)), ((), ())),
+            precision=lax.Precision.HIGHEST,
+            preferred_element_type=F32,
+        )
+        send_all(h, *stage1)
+        slots1[h, me1] = filt_local[rows_of(h, me1), :]
+
+    def after1(h):
+        await_part(h, *stage1)
+        acc1[h] = total(slots1, h, n_plane)
+        send_all(h, *stage2)
+        slots2[h, y] = acc1[h]
+
+    def after2(h):
+        await_part(h, *stage2)
+        acc2[h] = total(slots2, h, n_y)
+        send_all(h, *stage3)
+        slots3[h, me3] = acc2[h]
+
+    def after3(h):
+        await_part(h, *stage3)
+        acc3[h] = total(slots3, h, n_z)
+        send_all(h, *stage4)
+        gathered[h, me1] = acc3[h]
 
     lane_of = lax.broadcasted_iota(jnp.int32, (FILT, LANES), 1) // GSIZE
 
@@ -340,44 +379,73 @@
         gv[:, lanes] = (k[:, lanes].astype(F32) * grad).astype(BF16)
         return carry
 
-    send_all(*stage1)
-    slots1[me1] = filt_local[pl.ds(pl.multiple_of(me1 * share, share), share), :]
-    lax.fori_loop(0, tiles // 2, forward, 0)
-    await_all(*stage1, False)
-    acc1[...] = total(slots1, n_plane)
-    send_all(*stage2)
-    slots2[y] = acc1[...]
-    lax.fori_loop(tiles // 2, tiles, forward, 0)
-    stores = [
-        pltpu.make_async_copy(src, dst, out_sem.at[i])
-        for i, (src, dst) in enumerate(((mixed, mixed_hbm), (gq, gq_hbm), (gk, gk_hbm), (gv, gv_hbm)))
+    def chunks_of(first, end, size, ready, tile_work):
+        def one(i, carry):
+            ready(i)
+            return lax.fori_loop(i * size, (i + 1) * size, tile_work, carry)
+
+        lax.fori_loop(first, end, one, 0)
+
+    def kv_ready(i):
+        kv_copy(i).wait_recv()
+
+    def cot_ready(i):
+        cot_copy(i).wait_recv()
+
+    def tiles_of(part):
+        return (part * tiles) // 16
+
+    def run_forward(first, end):
+        lax.fori_loop(tiles_of(first), tiles_of(end), forward, 0)
+
+    def run_backward(first, end):
+        chunks_of(tiles_of(first) // COT_CHUNK, tiles_of(end) // COT_CHUNK, COT_CHUNK, cot_ready, backward)
+
+    chunks_of(0, part_chunks, CHUNK, kv_ready, products)
+    begin(0)
+    hear(0, z_near)
+    tell(1, z_far)
+    split = part_chunks + part_chunks // 2
+    chunks_of(part_chunks, split, CHUNK, kv_ready, products)
+    everything(kvs, kv_send, kv_recv.at[0]).wait_send()
+    for i in range(n_cot):
+        cot_copy(i).start()
+    chunks_of(split, n_chunks, CHUNK, kv_ready, products)
+    begin(1)
+    after1(0)
+    hear(1, z_far)
+    tell(2, z_far)
+    run_forward(0, 6)
+    after1(1)
+    run_forward(6, 14)
+    hear(2, z_far)
+    after2(0)
+    run_forward(14, 16)
+    run_backward(0, 4)
+    after2(1)
+    run_backward(4, 16)
+    after3(0)
+    after3(1)
+    everything(cots, cot_send, cot_recv.at[0]).wait_send()
+    for stage in (stage1, stage2, stage3):
+        await_sent(*stage)
+    for h in range(PARTS):
+        await_part(h, *stage4)
+    fg_ref[...] = gathered[...].reshape(fg_ref.shape) * scale
+    await_sent(*stage4)
+
+
+def write_out(*refs):
+    *ends, sem = refs
+    half = len(ends) // 2
+    copies = [
+        pltpu.make_async_copy(src, dst, sem.at[i])
+        for i, (src, dst) in enumerate(zip(ends[:half], ends[half:]))
     ]
-    stores[0].start()
-    stores[1].start()
-    await_all(*stage2, False)
-    acc2[...] = total(slots2, n_y)
-    send_all(*stage3)
-    slots3[me3] = acc2[...]
-    for i in range(n_chunks):
-        cot_copy(i).wait_recv()
-        lax.fori_loop(i * CHUNK, (i + 1) * CHUNK, backward, 0)
-    stores[2].start()
-    stores[3].start()
-    await_all(*stage3, False)
-    acc3[...] = total(slots3, n_z)
-    send_all(*stage4)
-    gathered[pl.ds(pl.multiple_of(me1 * share, share), share), :] = acc3[...]
-    for i in range(n_chunks):
-        kv_copy(i).wait_send()
-        cot_copy(i).wait_send()
-    await_all(*stage1, True)
-    await_all(*stage2, True)
-    await_all(*stage3, True)
-    for copy in stores:
+    for copy in copies:
+        copy.start()
+    for copy in copies:
         copy.wait()
-    await_all(*stage4, False)
-    fg_ref[...] = gathered[...] * scale
-    await_all(*stage4, True)
 
 
 def per_device(n_ctx, n_dp, q_proj, k_proj, v_proj, out_grad, contig_starts, filters):
@@ -387,19 +455,21 @@
     n_y = n_ctx // (CORES * Z_LO)
     n_plane = (n_dp // Z_HI) * CORES
     n_z = Z_LO * Z_HI
-    share = groups // n_plane
+    share = groups // (n_plane * PARTS)
     n_chunks = tiles // CHUNK
+    n_cot = tiles // COT_CHUNK
     scale = 1.0 / math.sqrt(rows * n_ctx * n_dp * GSIZE)
     any_spec = pl.BlockSpec(memory_space=pl.ANY)
     vmem_spec = pl.BlockSpec(memory_space=pltpu.VMEM)
+    small = jax.ShapeDtypeStruct((groups, FILT), F32)
     big = jax.ShapeDtypeStruct((rows, width), BF16)
     dma = pltpu.SemaphoreType.DMA
     wide = pltpu.VMEM((rows, width), BF16)
-    mixed, grad_q, grad_k, grad_v, filter_grad = pl.pallas_call(
+    results = pl.pallas_call(
         functools.partial(ring_kernel, n_ctx, n_dp, scale),
-        out_shape=(big, big, big, big, jax.ShapeDtypeStruct((groups, FILT), F32)),
+        out_shape=(wide, wide, wide, wide, pltpu.VMEM((groups, FILT), F32)),
         in_specs=[any_spec] * 4 + [vmem_spec] * 2,
-        out_specs=(any_spec, any_spec, any_spec, any_spec, vmem_spec),
+        out_specs=(vmem_spec,) * 5,
         scratch_shapes=[
             wide,
             wide,
@@ -418,34 +488,37 @@
             pltpu.VMEM((PER_TILE, SUB, FILT), F32),
             pltpu.VMEM((groups, FILT), F32),
             pltpu.VMEM((groups, FILT), F32),
-            pltpu.VMEM((n_plane, share, FILT), F32),
-            pltpu.VMEM((n_y, share, FILT), F32),
-            pltpu.VMEM((n_z, share, FILT), F32),
-            pltpu.VMEM((share, FILT), F32),
-            pltpu.VMEM((share, FILT), F32),
-            pltpu.VMEM((share, FILT), F32),
-            pltpu.VMEM((groups, FILT), F32),
-            wide,
-            wide,
-            wide,
-            wide,
+            pltpu.VMEM((PARTS, n_plane, share, FILT), F32),
+            pltpu.VMEM((PARTS, n_y, share, FILT), F32),
+            pltpu.VMEM((PARTS, n_z, share, FILT), F32),
+            pltpu.VMEM((PARTS, share, FILT), F32),
+            pltpu.VMEM((PARTS, share, FILT), F32),
+            pltpu.VMEM((PARTS, share, FILT), F32),
+            pltpu.VMEM((PARTS, n_plane, share, FILT), F32),
             dma((4,)),
-            dma((4,)),
+            dma(()),
             dma((n_chunks,)),
-            dma((n_chunks,)),
-            dma((n_chunks,)),
-            dma((n_chunks,)),
-            dma((n_plane,)),
-            dma((n_plane,)),
-            dma((n_y,)),
-            dma((n_y,)),
-            dma((n_z,)),
-            dma((n_z,)),
-            dma((n_plane,)),
-            dma((n_plane,)),
+            dma(()),
+            dma((n_cot,)),
+            dma(()),
+            dma((PARTS,)),
+            dma(()),
+            dma((PARTS,)),
+            dma(()),
+            dma((PARTS,)),
+            dma(()),
+            dma((PARTS,)),
+            pltpu.SemaphoreType.REGULAR((3,)),
         ],
         compiler_params=pltpu.CompilerParams(collective_id=0, has_side_effects=True),
     )(q_proj[0], k_proj[0], v_proj[0], out_grad[0], contig_starts, filters)
+    mixed, grad_q, grad_k, grad_v, filter_grad = pl.pallas_call(
+        write_out,
+        out_shape=(big, big, big, big, small),
+        in_specs=[vmem_spec] * 5,
+        out_specs=(any_spec,) * 5,
+        scratch_shapes=[dma((5,))],
+    )(*[pltpu.with_memory_space_constraint(r, pltpu.VMEM) for r in results])
     return (mixed[None], grad_q[None], grad_k[None], grad_v[None], filter_grad)
 
 

time: 60.7 us -> 52 us (0.86)
  local copies, waits for them, and re-layouts: 5.89 us -> 0 us
  Pallas kernels: 53.7 us -> 51.1 us
    unnamed x13 -> x0, local copies, waits for them, and re-layouts: 5.89 us -> none
    pallas_call x1, Pallas kernels: 53.7 us -> 49.8 us  [per_device(): pl.pallas_call(functools.partial(ring_kernel, n_ctx, n_dp, scale), out_sh...]
    pallas_call x0 -> x1, Pallas kernels: none -> 1.37 us  [per_device(): pl.pallas_call(write_out, out_shape=(big, big, big, big, small), in_specs...]
where the time goes in v2:
time: 52 us; the launch traced here: 51.8 us
  Pallas kernels  51.1 us (98%)
  between operations  0.64 us (1%)
    pallas_call x1, Pallas kernels, per_device(): pl.pallas_call(functools.partial(ring_kernel, n_ctx, n_dp, scale), out_sh...  49.8 us
    pallas_call x1, Pallas kernels, per_device(): pl.pallas_call(write_out, out_shape=(big, big, big, big, small), in_specs...  1.37 us

profile of v2, /device:TPU:1, one launch (start us, length us, event | category | flops | bytes accessed | tf_op | source)
XLA Modules:
  0.0 51.8 jit_solution(11508418719365710210)
XLA Ops:
  0.6 49.8 %shard_map.101 = (bf16[128,2048]{1,0:T(8,128)(2,1)S(1)}, bf16[128,2048]{1,0:T(8,128)(2,1)S(1)}, bf16[128,2048]{1,0:T(8,128)(2,1)S(1)}, bf16[128,2048]{1,0:T(8,128)(2,1)S(1)}, f32[128,128]{1,0:T(8,128)S(1)}) custom-call(bf16[128,2048]{1,0:T(8,128)(2,1)} %bitcast.8, bf16[128,2048]{1,0:T(8,128)(2,1)} %bitcast.9, bf16[128,2048]{1,0:T(8,128)(2,1)} %bitcast.10, ...), custom_call_target="tpu_custom_call" | custom-call | tf_op jit(solution)/shard_map/pallas_call | solution.py:468
  50.4 1.4 %shard_map.102 = (bf16[128,2048]{1,0:T(8,128)(2,1)}, bf16[128,2048]{1,0:T(8,128)(2,1)}, bf16[128,2048]{1,0:T(8,128)(2,1)}, bf16[128,2048]{1,0:T(8,128)(2,1)}, f32[128,128]{1,0:T(8,128)}) custom-call(bf16[128,2048]{1,0:T(8,128)(2,1)S(1)} %get-tuple-element.15.refs_0_, bf16[128,2048]{1,0:T(8,128)(2,1)S(1)} %get-tuple-element.16.refs_1_, ...), custom_call_target="tpu_custom_call" | custom-call | tf_op jit(solution)/shard_map/pallas_call | solution.py:515

commit v3 on v2

--- a/solution.py
+++ b/solution.py
@@ -48,6 +48,7 @@
     kvs,
     cots,
     lhs,
+    apart,
     lane_mask,
     masks,
     pair_mask,
@@ -135,19 +136,22 @@
     def z_step(d):
         return z_peer(lax.rem(me3 + d + n_z, n_z))
 
-    z_near = [d for d in (1, -1) if n_z > 1]
-    z_far = [d for d in (2, -2) if n_z > 3]
-    greet_all(n_y, y, y_peer)
+    def y_step(d):
+        return y_peer(lax.rem(y + d + n_y, n_y))
+
+    near = [(z_step, d) for d in (1, -1) if n_z > 1] + [(y_step, d) for d in (1, -1) if n_y > 1]
+    far = [(z_step, d) for d in (2, -2) if n_z > 3] + [(y_step, d) for d in (2, -2) if n_y > 3]
+    last = [(z_step, d) for d in (2, -2) if n_z > 3]
     greet(nxt)
     greet(prv)
-    for d in z_near:
-        greet(z_step(d))
+    for step, d in near:
+        greet(step(d))
     greet_all(n_plane, me1, plane_peer)
 
     def tell(stage, steps):
-        for d in steps:
+        for step, d in steps:
             pl.semaphore_signal(
-                heard.at[stage], inc=1, device_id=z_step(d), device_id_type=MESH
+                heard.at[stage], inc=1, device_id=step(d), device_id_type=MESH
             )
 
     def hear(stage, steps):
@@ -161,10 +165,10 @@
         jnp.sum(jnp.where(col <= row, starts, 0.0), axis=1, keepdims=True), (FILT, FILT)
     )
     seg_col = seg_row.T
-    last = jnp.sum(starts)
+    starts_sum = jnp.sum(starts)
     same = seg_row == seg_col
     fresh = seg_row == 0.0
-    final = seg_row == last
+    final = seg_row == starts_sum
 
     def held(cond):
         return jnp.where(cond, 1.0, 0.0)
@@ -201,7 +205,7 @@
 
     lax.fori_loop(0, tiles, make_kv, 0)
 
-    pl.semaphore_wait(barrier, 2 + len(z_near) + (n_y - 1) + (n_plane - 1))
+    pl.semaphore_wait(barrier, 2 + len(near) + (n_plane - 1))
 
     def kv_copy(i):
         part = pl.ds(i * CHUNK, CHUNK)
@@ -227,7 +231,7 @@
 
     for i in range(n_chunks):
         kv_copy(i).start()
-    tell(0, z_near)
+    tell(0, near)
 
     loads[2].wait()
     loads[3].wait()
@@ -237,16 +241,15 @@
         prod = (dy[:, lanes].astype(F32) * q[:, lanes].astype(F32)).astype(BF16)
         cotx[j, 0:FILT, :] = prod
         cots[j] = prod * masks[5]
+        for g in range(PER_TILE):
+            apart[j, g * FILT : (g + 1) * FILT, :] = prod * lane_mask[g]
         return carry
 
     lax.fori_loop(0, tiles, make_cot, 0)
 
-    def products(j, carry):
-        cot = cotx[j, 0:FILT, :]
-        for g in range(PER_TILE):
-            lhs[g * FILT : (g + 1) * FILT, 0:LANES] = cot * lane_mask[g]
+    def product_tile(j, where):
         pairs = lax.dot_general(
-            lhs[:, 0:LANES], kvx[j], (((1,), (1,)), ((), ())), preferred_element_type=F32
+            apart[j], kvx[j], (((1,), (1,)), ((), ())), preferred_element_type=F32
         )
         for g in range(PER_TILE):
             block = pairs[g * FILT : (g + 1) * FILT]
@@ -254,11 +257,15 @@
             folded = square[0:SUB]
             for a in range(1, FILT // SUB):
                 folded = folded + pltpu.roll(square[a * SUB : (a + 1) * SUB], FILT - a * SUB, 1)
-            fold[g] = folded
-        taps8 = fold[:, 0, :]
+            fold[where, g] = folded
+        taps8 = fold[where, :, 0, :]
         for b in range(1, SUB):
-            taps8 = taps8 + pltpu.roll(fold[:, b, :], FILT - b, 1)
+            taps8 = taps8 + pltpu.roll(fold[where, :, b, :], FILT - b, 1)
         filt_rev[pl.ds(pl.multiple_of(j * PER_TILE, PER_TILE), PER_TILE), :] = taps8
+
+    def products(i, carry):
+        for where in range(CHUNK):
+            product_tile(i * CHUNK + where, where)
         return carry
 
     def send_all(h, n, me, peer, src_of, dst, landed, send, recv):
@@ -401,24 +408,21 @@
     def run_backward(first, end):
         chunks_of(tiles_of(first) // COT_CHUNK, tiles_of(end) // COT_CHUNK, COT_CHUNK, cot_ready, backward)
 
-    chunks_of(0, part_chunks, CHUNK, kv_ready, products)
+    chunks_of(0, part_chunks, 1, kv_ready, products)
     begin(0)
-    hear(0, z_near)
-    tell(1, z_far)
-    split = part_chunks + part_chunks // 2
-    chunks_of(part_chunks, split, CHUNK, kv_ready, products)
-    everything(kvs, kv_send, kv_recv.at[0]).wait_send()
+    hear(0, near)
+    tell(1, far)
+    chunks_of(part_chunks, n_chunks, 1, kv_ready, products)
+    begin(1)
+    hear(1, far)
+    after1(0)
+    tell(2, last)
+    run_forward(0, 6)
+    after1(1)
     for i in range(n_cot):
         cot_copy(i).start()
-    chunks_of(split, n_chunks, CHUNK, kv_ready, products)
-    begin(1)
-    after1(0)
-    hear(1, z_far)
-    tell(2, z_far)
-    run_forward(0, 6)
-    after1(1)
     run_forward(6, 14)
-    hear(2, z_far)
+    hear(2, last)
     after2(0)
     run_forward(14, 16)
     run_backward(0, 4)
@@ -426,6 +430,7 @@
     run_backward(4, 16)
     after3(0)
     after3(1)
+    everything(kvs, kv_send, kv_recv.at[0]).wait_send()
     everything(cots, cot_send, cot_recv.at[0]).wait_send()
     for stage in (stage1, stage2, stage3):
         await_sent(*stage)
@@ -480,12 +485,13 @@
             pltpu.VMEM((tiles, FILT, LANES), BF16),
             pltpu.VMEM((tiles, FILT, LANES), BF16),
             pltpu.VMEM((PER_TILE * FILT, 2 * FILT), BF16),
+            pltpu.VMEM((tiles, PER_TILE * FILT, LANES), BF16),
             pltpu.VMEM((PER_TILE, FILT, LANES), BF16),
             pltpu.VMEM((6, FILT, FILT), BF16),
             pltpu.VMEM((FILT, FILT), F32),
             pltpu.VMEM((groups, FILT), F32),
             pltpu.VMEM((groups, FILT), F32),
-            pltpu.VMEM((PER_TILE, SUB, FILT), F32),
+            pltpu.VMEM((CHUNK, PER_TILE, SUB, FILT), F32),
             pltpu.VMEM((groups, FILT), F32),
             pltpu.VMEM((groups, FILT), F32),
             pltpu.VMEM((PARTS, n_plane, share, FILT), F32),

time: 52 us -> 51.4 us (0.988)
  Pallas kernels: 51.1 us -> 50.5 us
    pallas_call x1, Pallas kernels: 49.8 us -> 49.1 us  [per_device(): pl.pallas_call(functools.partial(ring_kernel, n_ctx, n_dp, scale), out_sh...]
where the time goes in v3:
time: 51.4 us; the launch traced here: 51.2 us
  Pallas kernels  50.5 us (98%)
  between operations  0.64 us (1%)
    pallas_call x1, Pallas kernels, per_device(): pl.pallas_call(functools.partial(ring_kernel, n_ctx, n_dp, scale), out_sh...  49.1 us
    pallas_call x1, Pallas kernels, per_device(): pl.pallas_call(write_out, out_shape=(big, big, big, big, small), in_specs...  1.37 us

profile of v3, /device:TPU:1, one launch (start us, length us, event | category | flops | bytes accessed | tf_op | source)
XLA Modules:
  0.0 51.2 jit_solution(15426878634730626320)
XLA Ops:
  0.6 49.1 %shard_map.101 = (bf16[128,2048]{1,0:T(8,128)(2,1)S(1)}, bf16[128,2048]{1,0:T(8,128)(2,1)S(1)}, bf16[128,2048]{1,0:T(8,128)(2,1)S(1)}, bf16[128,2048]{1,0:T(8,128)(2,1)S(1)}, f32[128,128]{1,0:T(8,128)S(1)}) custom-call(bf16[128,2048]{1,0:T(8,128)(2,1)} %bitcast.8, bf16[128,2048]{1,0:T(8,128)(2,1)} %bitcast.9, bf16[128,2048]{1,0:T(8,128)(2,1)} %bitcast.10, ...), custom_call_target="tpu_custom_call" | custom-call | tf_op jit(solution)/shard_map/pallas_call | solution.py:473
  49.8 1.4 %shard_map.102 = (bf16[128,2048]{1,0:T(8,128)(2,1)}, bf16[128,2048]{1,0:T(8,128)(2,1)}, bf16[128,2048]{1,0:T(8,128)(2,1)}, bf16[128,2048]{1,0:T(8,128)(2,1)}, f32[128,128]{1,0:T(8,128)}) custom-call(bf16[128,2048]{1,0:T(8,128)(2,1)S(1)} %get-tuple-element.15.refs_0_, bf16[128,2048]{1,0:T(8,128)(2,1)S(1)} %get-tuple-element.16.refs_1_, ...), custom_call_target="tpu_custom_call" | custom-call | tf_op jit(solution)/shard_map/pallas_call | solution.py:521

commit v4 on v3

--- a/solution.py
+++ b/solution.py
@@ -417,17 +417,17 @@
     hear(1, far)
     after1(0)
     tell(2, last)
-    run_forward(0, 6)
+    run_forward(0, 5)
     after1(1)
     for i in range(n_cot):
         cot_copy(i).start()
-    run_forward(6, 14)
+    run_forward(5, 11)
     hear(2, last)
     after2(0)
+    run_forward(11, 14)
+    after2(1)
     run_forward(14, 16)
-    run_backward(0, 4)
-    after2(1)
-    run_backward(4, 16)
+    run_backward(0, 16)
     after3(0)
     after3(1)
     everything(kvs, kv_send, kv_recv.at[0]).wait_send()

time: 51.4 us -> 51 us (level)
  no operation moved by 1% of the time
where the time goes in v4:
time: 51 us; the launch traced here: 50.8 us
  Pallas kernels  50.2 us (98%)
  between operations  0.64 us (1%)
    pallas_call x1, Pallas kernels, per_device(): pl.pallas_call(functools.partial(ring_kernel, n_ctx, n_dp, scale), out_sh...  48.8 us
    pallas_call x1, Pallas kernels, per_device(): pl.pallas_call(write_out, out_shape=(big, big, big, big, small), in_specs...  1.37 us

profile of v4, /device:TPU:1, one launch (start us, length us, event | category | flops | bytes accessed | tf_op | source)
XLA Modules:
  0.0 50.8 jit_solution(11689470265564598522)
XLA Ops:
  0.6 48.8 %shard_map.101 = (bf16[128,2048]{1,0:T(8,128)(2,1)S(1)}, bf16[128,2048]{1,0:T(8,128)(2,1)S(1)}, bf16[128,2048]{1,0:T(8,128)(2,1)S(1)}, bf16[128,2048]{1,0:T(8,128)(2,1)S(1)}, f32[128,128]{1,0:T(8,128)S(1)}) custom-call(bf16[128,2048]{1,0:T(8,128)(2,1)} %bitcast.8, bf16[128,2048]{1,0:T(8,128)(2,1)} %bitcast.9, bf16[128,2048]{1,0:T(8,128)(2,1)} %bitcast.10, ...), custom_call_target="tpu_custom_call" | custom-call | tf_op jit(solution)/shard_map/pallas_call | solution.py:473
  49.4 1.4 %shard_map.102 = (bf16[128,2048]{1,0:T(8,128)(2,1)}, bf16[128,2048]{1,0:T(8,128)(2,1)}, bf16[128,2048]{1,0:T(8,128)(2,1)}, bf16[128,2048]{1,0:T(8,128)(2,1)}, f32[128,128]{1,0:T(8,128)}) custom-call(bf16[128,2048]{1,0:T(8,128)(2,1)S(1)} %get-tuple-element.15.refs_0_, bf16[128,2048]{1,0:T(8,128)(2,1)S(1)} %get-tuple-element.16.refs_1_, ...), custom_call_target="tpu_custom_call" | custom-call | tf_op jit(solution)/shard_map/pallas_call | solution.py:521
